TPU v7x, 32 devices: a whole 2x2x4 slice. The times are simulated.
32 devices in a mesh: quad: 2 (over x), py: 4 (over y, core), pz: 4 (over z).
Axes of the slice: x: 2, y: 2, z: 4, core: 2. Of those that a mesh axis runs over, the one named last changes fastest.
Arguments:
- source_real: float32 [4, 16, 64, 512], P(None, None, 'py', 'pz'), may hold values from -6 to 6
- source_imag: float32 [4, 16, 64, 512], P(None, None, 'py', 'pz'), may hold values from -2 to 2
- potential: float32 [16, 64, 512], P(None, 'py', 'pz'), may hold values from 0 to 2
- center: float32 [1], replicated, may hold values from 4.5 to 6
- radius: float32 [1], replicated, may hold values from 1 to 2
Outputs:
- moments: float32 [4, 2, 4, 16, 64, 512], P(None, None, None, 'quad', 'py', 'pz')
All inputs are finite; a program needn't handle non-finite values.
Results may differ from a plain program's by a relative error of at most 0.0003.
Values sent between devices are 32-bit elements; how exact they have to be, the bound alone decides.
No kernel may reach another device: no remote copies, remote signals or barrier semaphores. Data moves between devices by JAX's collectives and lax.ppermute only.
A program may use at most 256 MiB of HBM per device.

v0:
```python
import math
import jax
import jax.numpy as jnp
from jax import lax
from jax.sharding import PartitionSpec as P

QPTS = 8
MOMS = 4
stencil_weights = (-205.0 / 72.0, 8.0 / 5.0, -1.0 / 5.0, 8.0 / 315.0, -1.0 / 560.0)


def padded_2(block, sides, width):
    for axis, dim in sides:
        count = lax.axis_size(axis)
        forward = [(i, i + 1) for i in range(count - 1)]
        forward.append((count - 1, 0))
        backward = [(target, source) for source, target in forward]
        low = lax.ppermute(
            lax.slice_in_dim(block, block.shape[dim] - width, None, axis=dim), axis, forward
        )
        high = lax.ppermute(lax.slice_in_dim(block, 0, width, axis=dim), axis, backward)
        block = jnp.concatenate([low, block, high], axis=dim)
    return block


def apply_operator(field, potential):
    padded = padded_2(field, (("py", 4), ("pz", 5)), 4)
    width_y = field.shape[4]
    width_z = field.shape[5]
    laplace = 3.0 * stencil_weights[0] * field
    for offset in range(1, 5):
        beside_all = jnp.roll(field, offset, 3) + jnp.roll(field, -offset, 3)
        beside_all = (
            beside_all + padded[:, :, :, :, 4 + offset : 4 + offset + width_y, 4 : 4 + width_z]
        )
        beside_all = (
            beside_all + padded[:, :, :, :, 4 - offset : 4 - offset + width_y, 4 : 4 + width_z]
        )
        beside_all = (
            beside_all + padded[:, :, :, :, 4 : 4 + width_y, 4 + offset : 4 + offset + width_z]
        )
        beside_all = (
            beside_all + padded[:, :, :, :, 4 : 4 + width_y, 4 - offset : 4 - offset + width_z]
        )
        laplace = laplace + stencil_weights[offset] * beside_all
    return -0.5 * laplace + potential * field


def complex_mul(left, right):
    return (left[0] * right[0] - left[1] * right[1], left[0] * right[1] + left[1] * right[0])


def complex_div(left, right):
    norm_sq = right[0] * right[0] + right[1] * right[1]
    return (
        (left[0] * right[0] + left[1] * right[1]) / norm_sq,
        (left[1] * right[0] - left[0] * right[1]) / norm_sq,
    )


def local_bilinear(left, right):
    both = complex_mul(left, right)
    return (jnp.sum(both[0], axis=(-3, -2, -1)), jnp.sum(both[1], axis=(-3, -2, -1)))


def spread(value):
    return (value[0][..., None, None, None], value[1][..., None, None, None])


def moment_terms(solution, angles, radius_value):
    orders = jnp.arange(1, MOMS + 1).astype(jnp.float32)
    phase = orders[:, None] * angles[None, :]
    weight_re = radius_value / QPTS * jnp.cos(phase)
    weight_im = radius_value / QPTS * jnp.sin(phase)
    highest = lax.Precision.HIGHEST
    real_part = jnp.einsum("kq,qsxyz->ksxyz", weight_re, solution[:, 0], precision=highest)
    real_part = real_part - jnp.einsum(
        "kq,qsxyz->ksxyz", weight_im, solution[:, 1], precision=highest
    )
    imag_part = jnp.einsum("kq,qsxyz->ksxyz", weight_re, solution[:, 1], precision=highest)
    imag_part = imag_part + jnp.einsum(
        "kq,qsxyz->ksxyz", weight_im, solution[:, 0], precision=highest
    )
    return jnp.stack([real_part, imag_part], 1)


def per_device(source_real, source_imag, potential, center, radius):
    groups = lax.axis_size("quad")
    local_count = QPTS // groups
    first_point = lax.axis_index("quad") * local_count
    indices = (first_point + jnp.arange(local_count)).astype(jnp.float32)
    angles = 2.0 * math.pi * (indices + 0.5) / QPTS
    shift_re = center[0] + radius[0] * jnp.cos(angles)
    shift_im = radius[0] * jnp.sin(angles)
    shift_pair = (shift_re[:, None], shift_im[:, None])
    shift_field = (shift_re[:, None, None, None, None], shift_im[:, None, None, None, None])
    source = (source_real, source_imag)
    applied = apply_operator(jnp.stack(source)[None], potential)[0]
    hsource = (applied[0], applied[1])
    rho_local = local_bilinear(source, source)
    curv_local = local_bilinear(source, hsource)
    totals = lax.psum((rho_local[0], rho_local[1], curv_local[0], curv_local[1]), ("py", "pz"))
    rho_first = (totals[0], totals[1])
    curv_first = (totals[2], totals[3])
    scaled = complex_mul(shift_pair, rho_first)
    denom = (scaled[0] - curv_first[0], scaled[1] - curv_first[1])
    alpha_first = complex_div(rho_first, denom)
    alpha_wide = spread(alpha_first)
    first_iterate = complex_mul(alpha_wide, source)
    shifted = complex_mul(shift_field, source)
    image = (shifted[0] - hsource[0], shifted[1] - hsource[1])
    moved = complex_mul(alpha_wide, image)
    residual = (source[0] - moved[0], source[1] - moved[1])
    hres = apply_operator(jnp.stack(residual, 1), potential)
    shifted_res = complex_mul(shift_field, residual)
    image_res = (shifted_res[0] - hres[:, 0], shifted_res[1] - hres[:, 1])
    rho_part = local_bilinear(residual, residual)
    mixed_part = local_bilinear(residual, image_res)
    paired = lax.psum((rho_part[0], rho_part[1], mixed_part[0], mixed_part[1]), ("py", "pz"))
    rho_next = (paired[0], paired[1])
    mixed = (paired[2], paired[3])
    beta = complex_div(rho_next, rho_first)
    carried = complex_mul(spread(beta), source)
    direction = (residual[0] + carried[0], residual[1] + carried[1])
    correction = complex_div(complex_mul(beta, rho_next), alpha_first)
    curv_next = (mixed[0] - correction[0], mixed[1] - correction[1])
    alpha_next = complex_div(rho_next, curv_next)
    step_part = complex_mul(spread(alpha_next), direction)
    solution = jnp.stack((first_iterate[0] + step_part[0], first_iterate[1] + step_part[1]), 1)
    terms = moment_terms(solution, angles, radius[0])
    return lax.psum_scatter(terms, "quad", scatter_dimension=3, tiled=True)


def solution(mesh):
    in_specs = (P(None, None, "py", "pz"), P(None, None, "py", "pz"), P(None, "py", "pz"), P(), P())
    out_specs = P(None, None, None, "quad", "py", "pz")
    return jax.shard_map(
        per_device, mesh=mesh, in_specs=in_specs, out_specs=out_specs, check_vma=False
    )
```

profile of v0, /device:TPU:0, one launch (start us, length us, event | category | flops | bytes accessed | tf_op | source)
XLA Modules:
  0.0 492.0 jit_solution(7060185690487794828)
XLA Ops:
  51.3 4.5 fusion.50
  63.6 17.7 %fusion.58 = f32[1,2,4,16,16,128]{5,4,3,2,1,0:T(8,128)S(1)} fusion(f32[1,2,4,16,24,4]{5,4,3,2,1,0:T(8,128)} %copy.96, f32[1,2,4,16,24,128]{5,4,3,2,1,0:T(8,128)} %copy.93, f32[1,2,4,16,24,4]{5,4,3,2,1,0:T(8,128)} %copy.94, f32[1,2,4,15,16,128]{5,4,3,2,1,0:T(8,128)} %copy.87, f32[1,2,4,1,16,128]{5,4,3,2,1,0:T(8,128)} %bitcast.76, ...), kind=kLoop, calls=%fused_computation.166 | loop fusion | flops 12845056 | bytes 20676608 | tf_op jit(solution)/shard_map/add | solution.py:46
  82.9 34.7 %all-reduce.1 = (f32[4]{0:T(128)S(1)}, f32[4]{0:T(128)S(1)}, f32[4]{0:T(128)S(1)}, f32[4]{0:T(128)S(1)}) all-reduce(f32[4]{0:T(128)S(1)} %get-tuple-element.10, f32[4]{0:T(128)S(1)} %get-tuple-element.9, f32[4]{0:T(128)S(1)} %get-tuple-element.12, f32[4]{0:T(128)S(1)} %get-tuple-element.11), channel_id=1, replica_groups=mesh['quad'=2,'py'=4,'pz'=4] {'py','pz'}, use_global_device_ids=true, to_apply=%region_7.8 | all-reduce | flops 16 | bytes 128 | tf_op jit(solution)/shard_map/psum | solution.py:102
  124.4 3.5 fusion.31
  133.6 19.1 %copy.121 = f32[4,2,4,16,16,128]{4,3,5,2,1,0:T(8,128)} copy(f32[4,2,4,16,16,128]{5,4,3,2,1,0:T(8,128)} %pad_maximum_fusion.1) | data formatting | bytes 8388608 | tf_op jit(solution)/shard_map/stack | solution.py:114
  155.3 3.4 fusion.29
  161.9 3.4 fusion.25
  165.4 18.9 %copy.122 = f32[4,2,4,16,4,128]{4,3,5,2,1,0:T(8,128)} copy(f32[4,2,4,16,4,128]{5,3,4,2,1,0:T(8,128)} %collective-permute-done.4) | data formatting | bytes 2097152 | tf_op jit(solution)/shard_map/ppermute | solution.py:21
  184.3 18.6 %copy.120 = f32[4,2,4,16,4,128]{4,3,5,2,1,0:T(8,128)} copy(f32[4,2,4,16,4,128]{5,3,4,2,1,0:T(8,128)} %collective-permute-done.5) | data formatting | bytes 2097152 | tf_op jit(solution)/shard_map/ppermute | solution.py:18
  202.9 43.9 %pad_maximum_fusion = f32[4,2,4,16,24,128]{4,3,5,2,1,0:T(8,128)} fusion(f32[4,2,4,16,4,128]{4,3,5,2,1,0:T(8,128)} %copy.122, f32[4,2,4,16,16,128]{4,3,5,2,1,0:T(8,128)} %copy.121, f32[4,2,4,16,4,128]{4,3,5,2,1,0:T(8,128)} %copy.120), kind=kLoop, calls=%fused_computation | loop fusion | flops 3145728 | bytes 12582912 | tf_op jit(solution)/shard_map/concatenate | solution.py:22
  249.9 4.0 collective-permute-start.6
  257.3 5.5 %pad_maximum_fusion.2 = (f32[4,2,4,16,20,128]{5,4,3,2,1,0:T(8,128)}, f32[4,2,4,16,20,128]{5,4,3,2,1,0:T(8,128)}) fusion(f32[4,2,4,16,4,128]{5,4,3,2,1,0:T(4,128)S(1)} %copy.117, f32[4,1,4,16,16,128]{5,4,3,2,1,0:T(8,128)S(1)} %get-tuple-element.48, f32[4,1,4,16,16,128]{5,4,3,2,1,0:T(8,128)S(1)} %copy-done.2, f32[4,2,4,16,4,128]{5,4,3,2,1,0:T(4,128)S(1)} %copy.119), kind=kLoop, calls=%fused_computation.50 | loop fusion | flops 5242880 | bytes 16777216 | tf_op jit(solution)/shard_map/concatenate | solution.py:22
  262.7 22.1 %copy.123 = f32[4,2,4,16,24,128]{5,4,3,2,1,0:T(8,128)} copy(f32[4,2,4,16,24,128]{4,3,5,2,1,0:T(8,128)} %pad_maximum_fusion) | data formatting | bytes 12582912 | tf_op jit(solution)/shard_map/concatenate | solution.py:22
  284.8 6.1 %copy.125 = f32[4,2,4,16,24,4]{5,4,3,2,1,0:T(8,128)} copy(f32[4,2,4,16,24,4]{4,3,5,2,1,0:T(8,128)} %collective-permute-done.7) | data formatting | bytes 393216 | tf_op jit(solution)/shard_map/ppermute | solution.py:18
  291.0 7.0 %collective-permute-done.6 = f32[4,2,4,16,24,4]{4,3,5,2,1,0:T(8,128)} collective-permute-done((f32[4,2,4,16,24,4]{4,3,5,2,1,0:T(8,128)}, f32[4,2,4,16,24,4]{4,3,5,2,1,0:T(8,128)}, u32[]{:S(2)}, u32[]{:S(2)}) %collective-permute-start.6) | collective-permute-done | bytes 196640 | tf_op jit(solution)/shard_map/ppermute | solution.py:21
  298.0 6.0 %copy.124 = f32[4,2,4,16,24,4]{5,4,3,2,1,0:T(8,128)} copy(f32[4,2,4,16,24,4]{4,3,5,2,1,0:T(8,128)} %collective-permute-done.6) | data formatting | bytes 393216 | tf_op jit(solution)/shard_map/ppermute | solution.py:21
  304.0 62.2 %fusion.6 = f32[4,2,4,16,16,128]{5,4,3,2,1,0:T(8,128)} fusion(f32[4,2,4,16,24,4]{5,4,3,2,1,0:T(8,128)} %copy.125, f32[4,2,4,16,24,128]{5,4,3,2,1,0:T(8,128)} %copy.123, f32[4,2,4,16,24,4]{5,4,3,2,1,0:T(8,128)} %copy.124, f32[4,2,4,16,20,128]{5,4,3,2,1,0:T(8,128)} %get-tuple-element.43, f32[4,2,4,16,20,128]{5,4,3,2,1,0:T(8,128)} %get-tuple-element.42, ...), kind=kLoop, calls=%fused_computation.70 | loop fusion | flops 51380224 | bytes 82313216 | tf_op jit(solution)/shard_map/add | solution.py:46
  366.3 5.0 %subtract_reduce_fusion = (f32[4,4]{1,0:T(4,128)S(1)}, f32[4,4]{1,0:T(4,128)S(1)}, f32[4,4]{1,0:T(4,128)S(1)}, f32[4,4]{1,0:T(4,128)S(1)}) fusion(f32[4,2,4,16,16,128]{5,4,3,2,1,0:T(8,128)} %fusion.6, f32[4]{0:T(128)S(1)} %get-tuple-element.88, f32[4]{0:T(128)S(1)} %get-tuple-element.89, f32[4,16,16,128]{3,2,1,0:T(8,128)S(1)} %copy-done.8, ...), kind=kLoop, calls=%fused_computation.129 | loop fusion | flops 20447168 | bytes 6291872 | tf_op jit(solution)/shard_map/reduce_sum | solution.py:63
  371.3 30.6 %all-reduce = (f32[4,4]{1,0:T(4,128)S(1)}, f32[4,4]{1,0:T(4,128)S(1)}, f32[4,4]{1,0:T(4,128)S(1)}, f32[4,4]{1,0:T(4,128)S(1)}) all-reduce(f32[4,4]{1,0:T(4,128)S(1)} %get-tuple-element.8, f32[4,4]{1,0:T(4,128)S(1)} %get-tuple-element.6, f32[4,4]{1,0:T(4,128)S(1)} %get-tuple-element.7, ...), channel_id=1, replica_groups=mesh['quad'=2,'py'=4,'pz'=4] {'py','pz'}, use_global_device_ids=true, to_apply=%region_9.10 | all-reduce | flops 64 | bytes 512 | tf_op jit(solution)/shard_map/psum | solution.py:119
  405.1 4.4 fusion.34
  409.5 4.4 fusion.36
  413.9 4.6 add_bitcast_fusion
  418.5 4.9 %subtract_bitcast_fusion = f32[4,1,4,16,16,128]{5,0,4,3,2,1:T(4,128)S(1)} fusion(f32[4,4,16,16,128]{4,0,3,2,1:T(4,128)S(1)} %fusion.36, f32[4,4,16,16,128]{4,3,2,1,0:T(8,128)S(1)} %get-tuple-element.46, f32[4]{0:T(128)S(1)} %copy-done.20, f32[4]{0:T(128)S(1)} %copy-done.21, f32[]{:T(128)S(6)} %div.49), kind=kOutput, calls=%fused_computation.123 | convolution fusion | flops 25690144 | bytes 6291492 | tf_op jit(solution)/shard_map/kq,qsxyz->ksxyz/dot_general | solution.py:76
  428.1 53.6 %reduce-scatter.2.cloned.1.call-done = f32[4,2,4,8,16,128]{5,4,2,1,0,3:T(8,128)} async-done(((f32[4,2,4,16,16,128]{5,4,2,1,0,3:T(8,128)}), f32[4,2,4,8,16,128]{5,4,2,1,0,3:T(8,128)}) %reduce-scatter.2.cloned.1.call-update) | async-done | bytes 2097168 | tf_op jit(solution)/shard_map/reduce_scatter | solution.py:131
  (136 shorter events, 88.3 us)
Async XLA Ops:
  6.5 475.1 %reduce-scatter.2.cloned.1.call-start = ((), (), s32[]{:S(2)}) async-start(), calls=%async_computation.1 | async-start | bytes 6291456 | tf_op jit(solution)/shard_map/reduce_scatter | solution.py:131
  9.0 28.6 %collective-permute-start = (f32[1,2,4,16,4,128]{5,3,4,2,1,0:T(8,128)}, f32[1,2,4,16,4,128]{5,3,4,2,1,0:T(8,128)}, u32[]{:S(2)}, u32[]{:S(2)}) collective-permute-start(f32[1,2,4,16,4,128]{5,3,4,2,1,0:T(8,128)} %get-tuple-element.83), channel_id=1, source_target_pairs={{4,0},{8,4},{12,8},{0,12},{5,1},{9,5},{13,9},{1,13},{6,2},{10,6},{... | collective-permute-start | bytes 786440 | tf_op jit(solution)/shard_map/ppermute | solution.py:21
  11.4 26.2 %collective-permute-start.1 = (f32[1,2,4,16,4,128]{5,3,4,2,1,0:T(8,128)}, f32[1,2,4,16,4,128]{5,3,4,2,1,0:T(8,128)}, u32[]{:S(2)}, u32[]{:S(2)}) collective-permute-start(f32[1,2,4,16,4,128]{5,3,4,2,1,0:T(8,128)} %get-tuple-element.82), channel_id=1, source_target_pairs={{0,4},{4,8},{8,12},{12,0},{1,5},{5,9},{9,13},{13,1},{2,6},{6,10},{... | collective-permute-start | bytes 786440 | tf_op jit(solution)/shard_map/ppermute | solution.py:18
  44.0 13.5 %collective-permute-start.3 = (f32[1,2,4,16,24,4]{4,3,5,2,1,0:T(8,128)}, f32[1,2,4,16,24,4]{4,3,5,2,1,0:T(8,128)}, u32[]{:S(2)}, u32[]{:S(2)}) collective-permute-start(f32[1,2,4,16,24,4]{4,3,5,2,1,0:T(8,128)} %copy.95), channel_id=1, source_target_pairs={{0,1},{1,2},{2,3},{3,0},{4,5},{5,6},{6,7},{7,4},{8,9},{9,10},{10,1... | collective-permute-start | bytes 147464 | tf_op jit(solution)/shard_map/ppermute | solution.py:18
  48.5 12.1 %collective-permute-start.2 = (f32[1,2,4,16,24,4]{4,3,5,2,1,0:T(8,128)}, f32[1,2,4,16,24,4]{4,3,5,2,1,0:T(8,128)}, u32[]{:S(2)}, u32[]{:S(2)}) collective-permute-start(f32[1,2,4,16,24,4]{4,3,5,2,1,0:T(8,128)} %copy.92), channel_id=1, source_target_pairs={{1,0},{2,1},{3,2},{0,3},{5,4},{6,5},{7,6},{4,7},{9,8},{10,9},{11,1... | collective-permute-start | bytes 147464 | tf_op jit(solution)/shard_map/ppermute | solution.py:21
  55.8 7.8 %copy-start.3 = (f32[4,16,16,128]{3,2,1,0:T(8,128)S(1)}, f32[4,16,16,128]{3,2,1,0:T(8,128)}, u32[]{:S(2)}) copy-start(f32[4,16,16,128]{3,2,1,0:T(8,128)} %param.6) | copy-start | bytes 1572868
  55.8 7.8 %copy-start.4 = (f32[4,16,16,128]{3,2,1,0:T(8,128)S(1)}, f32[4,16,16,128]{3,2,1,0:T(8,128)}, u32[]{:S(2)}) copy-start(f32[4,16,16,128]{3,2,1,0:T(8,128)} %param.5) | copy-start | bytes 1572868
  81.3 36.4 %copy-start.5 = (f32[4,16,16,128]{3,2,1,0:T(8,128)S(1)}, f32[4,16,16,128]{3,2,1,0:T(8,128)}, u32[]{:S(2)}) copy-start(f32[4,16,16,128]{3,2,1,0:T(8,128)} %param.5) | copy-start | bytes 1572868
  117.6 11.8 %copy-start.26 = (f32[4]{0:T(128)}, f32[4]{0:T(128)S(1)}, u32[]{:S(2)}) copy-start(f32[4]{0:T(128)S(1)} %get-tuple-element.19) | copy-start | bytes 52
  117.6 11.8 %copy-start.28 = (f32[4]{0:T(128)}, f32[4]{0:T(128)S(1)}, u32[]{:S(2)}) copy-start(f32[4]{0:T(128)S(1)} %get-tuple-element.20) | copy-start | bytes 52
  120.2 12.7 %copy-start = (f32[4,1,4,16,16,128]{5,4,3,2,1,0:T(8,128)}, f32[4,1,4,16,16,128]{5,4,3,2,1,0:T(8,128)S(1)}, u32[]{:S(2)}) copy-start(f32[4,1,4,16,16,128]{5,4,3,2,1,0:T(8,128)S(1)} %get-tuple-element.49) | copy-start | bytes 6291460
  131.1 34.3 %collective-permute-start.4 = (f32[4,2,4,16,4,128]{5,3,4,2,1,0:T(8,128)}, f32[4,2,4,16,4,128]{5,3,4,2,1,0:T(8,128)}, u32[]{:S(2)}, u32[]{:S(2)}) collective-permute-start(f32[4,2,4,16,4,128]{5,3,4,2,1,0:T(8,128)} %copy.144), channel_id=1, source_target_pairs={{4,0},{8,4},{12,8},{0,12},{5,1},{9,5},{13,9},{1,13},{6,2},{10,6},{... | collective-permute-start | bytes 3145736 | tf_op jit(solution)/shard_map/ppermute | solution.py:21
  132.2 52.1 %collective-permute-start.5 = (f32[4,2,4,16,4,128]{5,3,4,2,1,0:T(8,128)}, f32[4,2,4,16,4,128]{5,3,4,2,1,0:T(8,128)}, u32[]{:S(2)}, u32[]{:S(2)}) collective-permute-start(f32[4,2,4,16,4,128]{5,3,4,2,1,0:T(8,128)} %copy.145), channel_id=1, source_target_pairs={{0,4},{4,8},{8,12},{12,0},{1,5},{5,9},{9,13},{13,1},{2,6},{6,10},{... | collective-permute-start | bytes 3145736 | tf_op jit(solution)/shard_map/ppermute | solution.py:18
  249.9 34.9 %collective-permute-start.7 = (f32[4,2,4,16,24,4]{4,3,5,2,1,0:T(8,128)}, f32[4,2,4,16,24,4]{4,3,5,2,1,0:T(8,128)}, u32[]{:S(2)}, u32[]{:S(2)}) collective-permute-start(f32[4,2,4,16,24,4]{4,3,5,2,1,0:T(8,128)} %get-tuple-element.25), channel_id=1, source_target_pairs={{0,1},{1,2},{2,3},{3,0},{4,5},{5,6},{6,7},{7,4},{8,9},{9,10},{10,1... | collective-permute-start | bytes 589832 | tf_op jit(solution)/shard_map/ppermute | solution.py:18
  249.9 48.1 %collective-permute-start.6 = (f32[4,2,4,16,24,4]{4,3,5,2,1,0:T(8,128)}, f32[4,2,4,16,24,4]{4,3,5,2,1,0:T(8,128)}, u32[]{:S(2)}, u32[]{:S(2)}) collective-permute-start(f32[4,2,4,16,24,4]{4,3,5,2,1,0:T(8,128)} %get-tuple-element.24), channel_id=1, source_target_pairs={{1,0},{2,1},{3,2},{0,3},{5,4},{6,5},{7,6},{4,7},{9,8},{10,9},{11,1... | collective-permute-start | bytes 589832 | tf_op jit(solution)/shard_map/ppermute | solution.py:21
  304.0 62.2 %copy-start.6 = (f32[4,16,16,128]{3,2,1,0:T(8,128)S(1)}, f32[4,16,16,128]{3,2,1,0:T(8,128)}, u32[]{:S(2)}) copy-start(f32[4,16,16,128]{3,2,1,0:T(8,128)} %get-tuple-element.60) | copy-start | bytes 1572868
  304.0 62.2 %copy-start.8 = (f32[4,16,16,128]{3,2,1,0:T(8,128)S(1)}, f32[4,16,16,128]{3,2,1,0:T(8,128)}, u32[]{:S(2)}) copy-start(f32[4,16,16,128]{3,2,1,0:T(8,128)} %get-tuple-element.61) | copy-start | bytes 1572868
  366.3 35.7 %copy-start.23 = (f32[4]{0:T(128)S(1)}, f32[4]{0:T(128)}, u32[]{:S(2)}) copy-start(f32[4]{0:T(128)} %copy-done.22) | copy-start | bytes 52
  366.3 35.7 %copy-start.25 = (f32[4]{0:T(128)S(1)}, f32[4]{0:T(128)}, u32[]{:S(2)}) copy-start(f32[4]{0:T(128)} %copy-done.24) | copy-start | bytes 52
  366.3 35.7 %copy-start.27 = (f32[4]{0:T(128)S(1)}, f32[4]{0:T(128)}, u32[]{:S(2)}) copy-start(f32[4]{0:T(128)} %copy-done.26) | copy-start | bytes 52
  366.3 35.7 %copy-start.29 = (f32[4]{0:T(128)S(1)}, f32[4]{0:T(128)}, u32[]{:S(2)}) copy-start(f32[4]{0:T(128)} %copy-done.28) | copy-start | bytes 52
  366.3 35.7 %copy-start.30 = (f32[4]{0:T(128)S(1)}, f32[4]{0:T(128)}, u32[]{:S(2)}) copy-start(f32[4]{0:T(128)} %multiply_add_fusion.4) | copy-start | bytes 52
  366.3 35.8 %copy-start.7 = (f32[4,16,16,128]{3,2,1,0:T(8,128)S(1)}, f32[4,16,16,128]{3,2,1,0:T(8,128)}, u32[]{:S(2)}) copy-start(f32[4,16,16,128]{3,2,1,0:T(8,128)} %get-tuple-element.60) | copy-start | bytes 1572868
  366.3 35.8 %copy-start.9 = (f32[4,16,16,128]{3,2,1,0:T(8,128)S(1)}, f32[4,16,16,128]{3,2,1,0:T(8,128)}, u32[]{:S(2)}) copy-start(f32[4,16,16,128]{3,2,1,0:T(8,128)} %get-tuple-element.61) | copy-start | bytes 1572868
  (16 other events, 82.4 us)
Sparse Core Ops, SparseCore 0:
  428.2 53.3 reduce-scatter.1
where the time goes:
time: 499 us; the launch traced here: 492 us
  other arithmetic  173 us (35%)
  local copies, waits for them, and re-layouts  147 us (29%)
  blocking collectives  65.3 us (13%)
  waiting for transfers between devices  60.8 us (12%)
  matrix products  18.3 us (4%)
  between operations  15.5 us (3%)
  starting transfers between devices  11.4 us (2%)
    add x2, other arithmetic, apply_operator(): return -0.5 * laplace + potential * field  79.9 us
    concatenate x4, other arithmetic, padded_2(): block = jnp.concatenate([low, block, high], axis=dim)  55 us
    reduce_scatter x1, waiting for transfers between devices, per_device(): return lax.psum_scatter(terms, 'quad', scatter_dimension=3, tiled=True)  53.6 us
    psum x1, blocking collectives, per_device(): lax.psum((rho_local[0], rho_local[1], curv_local[0], curv_local[1]), ('py...  34.7 us
    psum x1, blocking collectives, per_device(): lax.psum((rho_part[0], rho_part[1], mixed_part[0], mixed_part[1]), ('py',...  30.6 us
    ppermute x4, local copies, waits for them, and re-layouts, padded_2(): lax.ppermute(lax.slice_in_dim(block, 0, width, axis=dim), axis, backward)  29.5 us
    ppermute x4, local copies, waits for them, and re-layouts, padded_2(): lax.ppermute(lax.slice_in_dim(block, block.shape[dim] - width, None, axis...  29.4 us
    concatenate x2, local copies, waits for them, and re-layouts, padded_2(): block = jnp.concatenate([low, block, high], axis=dim)  23.7 us
  transfers between devices with their start and end apart: 9, of which 3 were waited for; matrix products, arithmetic and copies ran while one was open for 26% of the time, Pallas kernels for 0%

commit v1 on v0

--- a/solution.py
+++ b/solution.py
@@ -116,7 +116,9 @@
     image_res = (shifted_res[0] - hres[:, 0], shifted_res[1] - hres[:, 1])
     rho_part = local_bilinear(residual, residual)
     mixed_part = local_bilinear(residual, image_res)
-    paired = lax.psum((rho_part[0], rho_part[1], mixed_part[0], mixed_part[1]), ("py", "pz"))
+    paired = lax.psum(
+        lax.psum((rho_part[0], rho_part[1], mixed_part[0], mixed_part[1]), "pz"), "py"
+    )
     rho_next = (paired[0], paired[1])
     mixed = (paired[2], paired[3])
     beta = complex_div(rho_next, rho_first)

time: 499 us -> 484 us (0.970)
  blocking collectives: 65.3 us -> 51.2 us
    psum x1 -> x2, blocking collectives: 30.6 us -> 16.5 us  [the longest x1 10.4 us: per_device(): lax.psum((rho_part[0], rho_part[1], mixed_part[0], mixed_part[1]), 'pz')]
where the time goes in v1:
time: 484 us; the launch traced here: 477 us
  other arithmetic  174 us (36%)
  local copies, waits for them, and re-layouts  147 us (30%)
  waiting for transfers between devices  59.1 us (12%)
  blocking collectives  51.2 us (11%)
  matrix products  18.3 us (4%)
  between operations  15.5 us (3%)
  starting transfers between devices  11.4 us (2%)
    add x2, other arithmetic, apply_operator(): return -0.5 * laplace + potential * field  80.9 us
    concatenate x4, other arithmetic, padded_2(): block = jnp.concatenate([low, block, high], axis=dim)  54.9 us
    reduce_scatter x1, waiting for transfers between devices, per_device(): return lax.psum_scatter(terms, 'quad', scatter_dimension=3, tiled=True)  51.8 us
    psum x1, blocking collectives, per_device(): lax.psum((rho_local[0], rho_local[1], curv_local[0], curv_local[1]), ('py...  34.7 us
    ppermute x4, local copies, waits for them, and re-layouts, padded_2(): lax.ppermute(lax.slice_in_dim(block, 0, width, axis=dim), axis, backward)  29.5 us
    ppermute x4, local copies, waits for them, and re-layouts, padded_2(): lax.ppermute(lax.slice_in_dim(block, block.shape[dim] - width, None, axis...  29.4 us
    concatenate x2, local copies, waits for them, and re-layouts, padded_2(): block = jnp.concatenate([low, block, high], axis=dim)  23.7 us
    slice x22, local copies, waits for them, and re-layouts, apply_operator(): beside_all = jnp.roll(field, offset, 3) + jnp.roll(field, -offset, 3)  23.7 us
  transfers between devices with their start and end apart: 9, of which 3 were waited for; matrix products, arithmetic and copies ran while one was open for 26% of the time, Pallas kernels for 0%

profile of v1, /device:TPU:0, one launch (start us, length us, event | category | flops | bytes accessed | tf_op | source)
XLA Modules:
  0.0 477.0 jit_solution(3406231870584111403)
XLA Ops:
  51.3 4.5 fusion.50
  63.6 17.9 %fusion.58 = f32[1,2,4,16,16,128]{5,4,3,2,1,0:T(8,128)S(1)} fusion(f32[1,2,4,16,24,4]{5,4,3,2,1,0:T(8,128)} %copy.96, f32[1,2,4,16,24,128]{5,4,3,2,1,0:T(8,128)} %copy.93, f32[1,2,4,16,24,4]{5,4,3,2,1,0:T(8,128)} %copy.94, f32[1,2,4,15,16,128]{5,4,3,2,1,0:T(8,128)} %copy.87, f32[1,2,4,1,16,128]{5,4,3,2,1,0:T(8,128)} %bitcast.76, ...), kind=kLoop, calls=%fused_computation.166 | loop fusion | flops 12845056 | bytes 20676608 | tf_op jit(solution)/shard_map/add | solution.py:46
  83.0 34.7 %all-reduce = (f32[4]{0:T(128)S(1)}, f32[4]{0:T(128)S(1)}, f32[4]{0:T(128)S(1)}, f32[4]{0:T(128)S(1)}) all-reduce(f32[4]{0:T(128)S(1)} %get-tuple-element.10, f32[4]{0:T(128)S(1)} %get-tuple-element.9, f32[4]{0:T(128)S(1)} %get-tuple-element.12, f32[4]{0:T(128)S(1)} %get-tuple-element.11), channel_id=1, replica_groups=mesh['quad'=2,'py'=4,'pz'=4] {'py','pz'}, use_global_device_ids=true, to_apply=%region_7.8 | all-reduce | flops 16 | bytes 128 | tf_op jit(solution)/shard_map/psum | solution.py:102
  124.4 3.5 fusion.31
  133.7 19.1 %copy.121 = f32[4,2,4,16,16,128]{4,3,5,2,1,0:T(8,128)} copy(f32[4,2,4,16,16,128]{5,4,3,2,1,0:T(8,128)} %pad_maximum_fusion.1) | data formatting | bytes 8388608 | tf_op jit(solution)/shard_map/stack | solution.py:114
  162.0 3.4 fusion.25
  165.5 18.9 %copy.122 = f32[4,2,4,16,4,128]{4,3,5,2,1,0:T(8,128)} copy(f32[4,2,4,16,4,128]{5,3,4,2,1,0:T(8,128)} %collective-permute-done.4) | data formatting | bytes 2097152 | tf_op jit(solution)/shard_map/ppermute | solution.py:21
  184.4 18.6 %copy.120 = f32[4,2,4,16,4,128]{4,3,5,2,1,0:T(8,128)} copy(f32[4,2,4,16,4,128]{5,3,4,2,1,0:T(8,128)} %collective-permute-done.5) | data formatting | bytes 2097152 | tf_op jit(solution)/shard_map/ppermute | solution.py:18
  202.9 43.9 %pad_maximum_fusion = f32[4,2,4,16,24,128]{4,3,5,2,1,0:T(8,128)} fusion(f32[4,2,4,16,4,128]{4,3,5,2,1,0:T(8,128)} %copy.122, f32[4,2,4,16,16,128]{4,3,5,2,1,0:T(8,128)} %copy.121, f32[4,2,4,16,4,128]{4,3,5,2,1,0:T(8,128)} %copy.120), kind=kLoop, calls=%fused_computation | loop fusion | flops 3145728 | bytes 12582912 | tf_op jit(solution)/shard_map/concatenate | solution.py:22
  250.0 4.0 collective-permute-start.6
  257.3 5.5 %pad_maximum_fusion.2 = (f32[4,2,4,16,20,128]{5,4,3,2,1,0:T(8,128)}, f32[4,2,4,16,20,128]{5,4,3,2,1,0:T(8,128)}) fusion(f32[4,2,4,16,4,128]{5,4,3,2,1,0:T(4,128)S(1)} %copy.117, f32[4,1,4,16,16,128]{5,4,3,2,1,0:T(8,128)S(1)} %get-tuple-element.52, f32[4,1,4,16,16,128]{5,4,3,2,1,0:T(8,128)S(1)} %copy-done.2, f32[4,2,4,16,4,128]{5,4,3,2,1,0:T(4,128)S(1)} %copy.119), kind=kLoop, calls=%fused_computation.50 | loop fusion | flops 5242880 | bytes 16777216 | tf_op jit(solution)/shard_map/concatenate | solution.py:22
  262.7 22.1 %copy.123 = f32[4,2,4,16,24,128]{5,4,3,2,1,0:T(8,128)} copy(f32[4,2,4,16,24,128]{4,3,5,2,1,0:T(8,128)} %pad_maximum_fusion) | data formatting | bytes 12582912 | tf_op jit(solution)/shard_map/concatenate | solution.py:22
  284.8 6.1 %copy.125 = f32[4,2,4,16,24,4]{5,4,3,2,1,0:T(8,128)} copy(f32[4,2,4,16,24,4]{4,3,5,2,1,0:T(8,128)} %collective-permute-done.7) | data formatting | bytes 393216 | tf_op jit(solution)/shard_map/ppermute | solution.py:18
  290.9 7.1 %collective-permute-done.6 = f32[4,2,4,16,24,4]{4,3,5,2,1,0:T(8,128)} collective-permute-done((f32[4,2,4,16,24,4]{4,3,5,2,1,0:T(8,128)}, f32[4,2,4,16,24,4]{4,3,5,2,1,0:T(8,128)}, u32[]{:S(2)}, u32[]{:S(2)}) %collective-permute-start.6) | collective-permute-done | bytes 196640 | tf_op jit(solution)/shard_map/ppermute | solution.py:21
  298.0 6.0 %copy.124 = f32[4,2,4,16,24,4]{5,4,3,2,1,0:T(8,128)} copy(f32[4,2,4,16,24,4]{4,3,5,2,1,0:T(8,128)} %collective-permute-done.6) | data formatting | bytes 393216 | tf_op jit(solution)/shard_map/ppermute | solution.py:21
  304.1 63.1 %fusion.6 = f32[4,2,4,16,16,128]{5,4,3,2,1,0:T(8,128)} fusion(f32[4,2,4,16,24,4]{5,4,3,2,1,0:T(8,128)} %copy.125, f32[4,2,4,16,24,128]{5,4,3,2,1,0:T(8,128)} %copy.123, f32[4,2,4,16,24,4]{5,4,3,2,1,0:T(8,128)} %copy.124, f32[4,2,4,16,20,128]{5,4,3,2,1,0:T(8,128)} %get-tuple-element.47, f32[4,2,4,16,20,128]{5,4,3,2,1,0:T(8,128)} %get-tuple-element.46, ...), kind=kLoop, calls=%fused_computation.70 | loop fusion | flops 51380224 | bytes 82313216 | tf_op jit(solution)/shard_map/add | solution.py:46
  367.2 5.0 %subtract_reduce_fusion = (f32[4,4]{1,0:T(4,128)S(1)}, f32[4,4]{1,0:T(4,128)S(1)}, f32[4,4]{1,0:T(4,128)S(1)}, f32[4,4]{1,0:T(4,128)S(1)}) fusion(f32[4,2,4,16,16,128]{5,4,3,2,1,0:T(8,128)} %fusion.6, f32[4]{0:T(128)S(1)} %get-tuple-element.92, f32[4]{0:T(128)S(1)} %get-tuple-element.93, f32[4,16,16,128]{3,2,1,0:T(8,128)S(1)} %copy-done.8, ...), kind=kLoop, calls=%fused_computation.129 | loop fusion | flops 20447168 | bytes 6291872 | tf_op jit(solution)/shard_map/reduce_sum | solution.py:63
  372.2 10.4 %all-reduce.1 = (f32[4,4]{1,0:T(4,128)S(1)}, f32[4,4]{1,0:T(4,128)S(1)}, f32[4,4]{1,0:T(4,128)S(1)}, f32[4,4]{1,0:T(4,128)S(1)}) all-reduce(f32[4,4]{1,0:T(4,128)S(1)} %get-tuple-element.8, f32[4,4]{1,0:T(4,128)S(1)} %get-tuple-element.6, f32[4,4]{1,0:T(4,128)S(1)} %get-tuple-element.7, ...), channel_id=1, replica_groups=mesh['quad'=2,'py'=4,'pz'=4] {'pz'}, use_global_device_ids=true, to_apply=%region_9.10 | all-reduce | flops 64 | bytes 512 | tf_op jit(solution)/shard_map/psum | solution.py:120
  382.6 6.1 %all-reduce.2 = (f32[4,4]{1,0:T(4,128)S(1)}, f32[4,4]{1,0:T(4,128)S(1)}, f32[4,4]{1,0:T(4,128)S(1)}, f32[4,4]{1,0:T(4,128)S(1)}) all-reduce(f32[4,4]{1,0:T(4,128)S(1)} %get-tuple-element.17, f32[4,4]{1,0:T(4,128)S(1)} %get-tuple-element.18, f32[4,4]{1,0:T(4,128)S(1)} %get-tuple-element.19, ...), channel_id=1, replica_groups=mesh['quad'=2,'py'=4,'pz'=4] {'py'}, use_global_device_ids=true, to_apply=%region_10.11 | all-reduce | flops 64 | bytes 512 | tf_op jit(solution)/shard_map/psum | solution.py:119
  391.8 4.4 fusion.34
  396.2 4.4 fusion.36
  400.6 4.6 add_bitcast_fusion
  405.2 4.9 %subtract_bitcast_fusion = f32[4,1,4,16,16,128]{5,0,4,3,2,1:T(4,128)S(1)} fusion(f32[4,4,16,16,128]{4,0,3,2,1:T(4,128)S(1)} %fusion.36, f32[4,4,16,16,128]{4,3,2,1,0:T(8,128)S(1)} %get-tuple-element.50, f32[4]{0:T(128)S(1)} %copy-done.20, f32[4]{0:T(128)S(1)} %copy-done.21, f32[]{:T(128)S(6)} %div.49), kind=kOutput, calls=%fused_computation.123 | convolution fusion | flops 25690144 | bytes 6291492 | tf_op jit(solution)/shard_map/kq,qsxyz->ksxyz/dot_general | solution.py:76
  414.8 51.8 %reduce-scatter.2.cloned.1.call-done = f32[4,2,4,8,16,128]{5,4,2,1,0,3:T(8,128)} async-done(((f32[4,2,4,16,16,128]{5,4,2,1,0,3:T(8,128)}), f32[4,2,4,8,16,128]{5,4,2,1,0,3:T(8,128)}) %reduce-scatter.2.cloned.1.call-update) | async-done | bytes 2097168 | tf_op jit(solution)/shard_map/reduce_scatter | solution.py:133
  (137 shorter events, 91.7 us)
Async XLA Ops:
  6.5 460.1 %reduce-scatter.2.cloned.1.call-start = ((), (), s32[]{:S(2)}) async-start(), calls=%async_computation.1 | async-start | bytes 6291456 | tf_op jit(solution)/shard_map/reduce_scatter | solution.py:133
  9.0 28.6 %collective-permute-start = (f32[1,2,4,16,4,128]{5,3,4,2,1,0:T(8,128)}, f32[1,2,4,16,4,128]{5,3,4,2,1,0:T(8,128)}, u32[]{:S(2)}, u32[]{:S(2)}) collective-permute-start(f32[1,2,4,16,4,128]{5,3,4,2,1,0:T(8,128)} %get-tuple-element.87), channel_id=1, source_target_pairs={{4,0},{8,4},{12,8},{0,12},{5,1},{9,5},{13,9},{1,13},{6,2},{10,6},{... | collective-permute-start | bytes 786440 | tf_op jit(solution)/shard_map/ppermute | solution.py:21
  11.4 26.2 %collective-permute-start.1 = (f32[1,2,4,16,4,128]{5,3,4,2,1,0:T(8,128)}, f32[1,2,4,16,4,128]{5,3,4,2,1,0:T(8,128)}, u32[]{:S(2)}, u32[]{:S(2)}) collective-permute-start(f32[1,2,4,16,4,128]{5,3,4,2,1,0:T(8,128)} %get-tuple-element.86), channel_id=1, source_target_pairs={{0,4},{4,8},{8,12},{12,0},{1,5},{5,9},{9,13},{13,1},{2,6},{6,10},{... | collective-permute-start | bytes 786440 | tf_op jit(solution)/shard_map/ppermute | solution.py:18
  44.0 13.5 %collective-permute-start.3 = (f32[1,2,4,16,24,4]{4,3,5,2,1,0:T(8,128)}, f32[1,2,4,16,24,4]{4,3,5,2,1,0:T(8,128)}, u32[]{:S(2)}, u32[]{:S(2)}) collective-permute-start(f32[1,2,4,16,24,4]{4,3,5,2,1,0:T(8,128)} %copy.95), channel_id=1, source_target_pairs={{0,1},{1,2},{2,3},{3,0},{4,5},{5,6},{6,7},{7,4},{8,9},{9,10},{10,1... | collective-permute-start | bytes 147464 | tf_op jit(solution)/shard_map/ppermute | solution.py:18
  48.5 12.1 %collective-permute-start.2 = (f32[1,2,4,16,24,4]{4,3,5,2,1,0:T(8,128)}, f32[1,2,4,16,24,4]{4,3,5,2,1,0:T(8,128)}, u32[]{:S(2)}, u32[]{:S(2)}) collective-permute-start(f32[1,2,4,16,24,4]{4,3,5,2,1,0:T(8,128)} %copy.92), channel_id=1, source_target_pairs={{1,0},{2,1},{3,2},{0,3},{5,4},{6,5},{7,6},{4,7},{9,8},{10,9},{11,1... | collective-permute-start | bytes 147464 | tf_op jit(solution)/shard_map/ppermute | solution.py:21
  55.8 7.8 %copy-start.3 = (f32[4,16,16,128]{3,2,1,0:T(8,128)S(1)}, f32[4,16,16,128]{3,2,1,0:T(8,128)}, u32[]{:S(2)}) copy-start(f32[4,16,16,128]{3,2,1,0:T(8,128)} %param.6) | copy-start | bytes 1572868
  55.8 7.8 %copy-start.4 = (f32[4,16,16,128]{3,2,1,0:T(8,128)S(1)}, f32[4,16,16,128]{3,2,1,0:T(8,128)}, u32[]{:S(2)}) copy-start(f32[4,16,16,128]{3,2,1,0:T(8,128)} %param.5) | copy-start | bytes 1572868
  81.4 36.4 %copy-start.5 = (f32[4,16,16,128]{3,2,1,0:T(8,128)S(1)}, f32[4,16,16,128]{3,2,1,0:T(8,128)}, u32[]{:S(2)}) copy-start(f32[4,16,16,128]{3,2,1,0:T(8,128)} %param.5) | copy-start | bytes 1572868
  117.7 11.9 %copy-start.26 = (f32[4]{0:T(128)}, f32[4]{0:T(128)S(1)}, u32[]{:S(2)}) copy-start(f32[4]{0:T(128)S(1)} %get-tuple-element.15) | copy-start | bytes 52
  117.7 11.8 %copy-start.28 = (f32[4]{0:T(128)}, f32[4]{0:T(128)S(1)}, u32[]{:S(2)}) copy-start(f32[4]{0:T(128)S(1)} %get-tuple-element.16) | copy-start | bytes 52
  120.3 12.7 %copy-start = (f32[4,1,4,16,16,128]{5,4,3,2,1,0:T(8,128)}, f32[4,1,4,16,16,128]{5,4,3,2,1,0:T(8,128)S(1)}, u32[]{:S(2)}) copy-start(f32[4,1,4,16,16,128]{5,4,3,2,1,0:T(8,128)S(1)} %get-tuple-element.53) | copy-start | bytes 6291460
  131.2 34.3 %collective-permute-start.4 = (f32[4,2,4,16,4,128]{5,3,4,2,1,0:T(8,128)}, f32[4,2,4,16,4,128]{5,3,4,2,1,0:T(8,128)}, u32[]{:S(2)}, u32[]{:S(2)}) collective-permute-start(f32[4,2,4,16,4,128]{5,3,4,2,1,0:T(8,128)} %copy.144), channel_id=1, source_target_pairs={{4,0},{8,4},{12,8},{0,12},{5,1},{9,5},{13,9},{1,13},{6,2},{10,6},{... | collective-permute-start | bytes 3145736 | tf_op jit(solution)/shard_map/ppermute | solution.py:21
  132.3 52.1 %collective-permute-start.5 = (f32[4,2,4,16,4,128]{5,3,4,2,1,0:T(8,128)}, f32[4,2,4,16,4,128]{5,3,4,2,1,0:T(8,128)}, u32[]{:S(2)}, u32[]{:S(2)}) collective-permute-start(f32[4,2,4,16,4,128]{5,3,4,2,1,0:T(8,128)} %copy.145), channel_id=1, source_target_pairs={{0,4},{4,8},{8,12},{12,0},{1,5},{5,9},{9,13},{13,1},{2,6},{6,10},{... | collective-permute-start | bytes 3145736 | tf_op jit(solution)/shard_map/ppermute | solution.py:18
  250.0 34.9 %collective-permute-start.7 = (f32[4,2,4,16,24,4]{4,3,5,2,1,0:T(8,128)}, f32[4,2,4,16,24,4]{4,3,5,2,1,0:T(8,128)}, u32[]{:S(2)}, u32[]{:S(2)}) collective-permute-start(f32[4,2,4,16,24,4]{4,3,5,2,1,0:T(8,128)} %get-tuple-element.29), channel_id=1, source_target_pairs={{0,1},{1,2},{2,3},{3,0},{4,5},{5,6},{6,7},{7,4},{8,9},{9,10},{10,1... | collective-permute-start | bytes 589832 | tf_op jit(solution)/shard_map/ppermute | solution.py:18
  250.0 48.1 %collective-permute-start.6 = (f32[4,2,4,16,24,4]{4,3,5,2,1,0:T(8,128)}, f32[4,2,4,16,24,4]{4,3,5,2,1,0:T(8,128)}, u32[]{:S(2)}, u32[]{:S(2)}) collective-permute-start(f32[4,2,4,16,24,4]{4,3,5,2,1,0:T(8,128)} %get-tuple-element.28), channel_id=1, source_target_pairs={{1,0},{2,1},{3,2},{0,3},{5,4},{6,5},{7,6},{4,7},{9,8},{10,9},{11,1... | collective-permute-start | bytes 589832 | tf_op jit(solution)/shard_map/ppermute | solution.py:21
  304.1 63.1 %copy-start.6 = (f32[4,16,16,128]{3,2,1,0:T(8,128)S(1)}, f32[4,16,16,128]{3,2,1,0:T(8,128)}, u32[]{:S(2)}) copy-start(f32[4,16,16,128]{3,2,1,0:T(8,128)} %get-tuple-element.64) | copy-start | bytes 1572868
  304.1 63.1 %copy-start.8 = (f32[4,16,16,128]{3,2,1,0:T(8,128)S(1)}, f32[4,16,16,128]{3,2,1,0:T(8,128)}, u32[]{:S(2)}) copy-start(f32[4,16,16,128]{3,2,1,0:T(8,128)} %get-tuple-element.65) | copy-start | bytes 1572868
  367.1 21.5 %copy-start.23 = (f32[4]{0:T(128)S(1)}, f32[4]{0:T(128)}, u32[]{:S(2)}) copy-start(f32[4]{0:T(128)} %copy-done.22) | copy-start | bytes 52
  367.2 21.5 %copy-start.25 = (f32[4]{0:T(128)S(1)}, f32[4]{0:T(128)}, u32[]{:S(2)}) copy-start(f32[4]{0:T(128)} %copy-done.24) | copy-start | bytes 52
  367.2 21.5 %copy-start.27 = (f32[4]{0:T(128)S(1)}, f32[4]{0:T(128)}, u32[]{:S(2)}) copy-start(f32[4]{0:T(128)} %copy-done.26) | copy-start | bytes 52
  367.2 21.5 %copy-start.29 = (f32[4]{0:T(128)S(1)}, f32[4]{0:T(128)}, u32[]{:S(2)}) copy-start(f32[4]{0:T(128)} %copy-done.28) | copy-start | bytes 52
  367.2 21.5 %copy-start.30 = (f32[4]{0:T(128)S(1)}, f32[4]{0:T(128)}, u32[]{:S(2)}) copy-start(f32[4]{0:T(128)} %multiply_add_fusion.4) | copy-start | bytes 52
  367.2 21.6 %copy-start.7 = (f32[4,16,16,128]{3,2,1,0:T(8,128)S(1)}, f32[4,16,16,128]{3,2,1,0:T(8,128)}, u32[]{:S(2)}) copy-start(f32[4,16,16,128]{3,2,1,0:T(8,128)} %get-tuple-element.64) | copy-start | bytes 1572868
  367.2 21.6 %copy-start.9 = (f32[4,16,16,128]{3,2,1,0:T(8,128)S(1)}, f32[4,16,16,128]{3,2,1,0:T(8,128)}, u32[]{:S(2)}) copy-start(f32[4,16,16,128]{3,2,1,0:T(8,128)} %get-tuple-element.65) | copy-start | bytes 1572868
  (16 other events, 82.4 us)
Sparse Core Ops, SparseCore 0:
  414.9 51.6 reduce-scatter.1
